TPU v7x, 128 devices: a whole 4x4x4 slice. The times are simulated.
128 devices in a mesh: patch: 32 (over y, z, x_lo), level: 4 (over x_hi, core).
Axes of the slice: x: 4 (x_hi: 2, x_lo: 2; x = x_hi * 2 + x_lo), y: 4, z: 4, core: 2. Of those that a mesh axis runs over, the one named last changes fastest.
Arguments:
- fields: float32 [6, 64, 32768], P(None, None, ('patch', 'level')), may hold values from -6 to 6
- inv_jacobian: float32 [32768], P(('patch', 'level')), may hold values from 0.5 to 2
- diff_matrix: float32 [3, 64, 64], replicated, may hold values from -0.75 to 0.75
- face_interp: float32 [6, 16, 64], replicated, may hold values from -0.75 to 0.75
- lift_matrix: float32 [6, 64, 16], replicated, may hold values from -1.5 to 1.5
- flux_couple: float32 [6, 6, 6], replicated, may hold values from -2.5 to 2.5
- neighbours: int32 [6, 32768], P(None, ('patch', 'level')), may hold values from 0 to 287
- send_index: int32 [2, 2048], P(None, ('patch', 'level')), may hold values from 0 to 255
- bound_coef: float32 [6], replicated, may hold values from 0.5 to 1.5
- current_coef: float32 [6], replicated, may hold values from -1 to 1
- time_interp: float32 [64], replicated, may hold values from -2 to 2
- current_history: bfloat16 [64, 16384], P(None, ('patch', 'level')), may hold values from -6 to 6
- group_weight: bfloat16 [128, 16384], P(None, ('patch', 'level')), may hold values from -0.1875 to 0.1875
- projection: bfloat16 [16384, 512], P(('patch', 'level')), may hold values from -6 to 6
- kernels: bfloat16 [4, 32, 16, 64], P('level', 'patch'), may hold values from -0.75 to 0.75
- pair_dest: int32 [4, 32, 16], P('level', 'patch'), may hold values from 0 to 31, as said below
- pair_count: int32 [4, 32], P('level', 'patch'), may hold values from 8 to 16
Outputs:
- field_rate: float32 [6, 64, 32768], P(None, None, ('patch', 'level'))
- boundary_field: float32 [64, 16384], P(None, ('patch', 'level'))
Inputs may be any that keep to these rules, and one draw needn't show every extreme that they name: `pair_dest`: in each row the 16 entries are distinct patches, none the row's own patch. Only the first pair_count slots of a group are live. `neighbours`: indices below 256 are the device's own elements, then 16 ghosts from the device below and 16 from the device above along patch+level, wrapping. `send_index`: local element indices of the device.
All inputs are finite; a program needn't handle non-finite values.
Results may differ from a plain program's by a relative error of at most 0.0049.
Values may be sent and summed in bfloat16 or wider, within the bound.
No kernel may reach another device: no remote copies, remote signals or barrier semaphores. Data moves between devices by JAX's collectives and lax.ppermute only.
A program may use at most 192 MiB of HBM per device.

v0:
```python
import math
import jax
import jax.numpy as jnp
from jax import lax
from jax.sharding import PartitionSpec as P

NFP = 16
BE = 8
HIGH = lax.Precision.HIGHEST


def padded_2(array, sides, width):
    edges = {}
    for axis, dim in sides:
        size, length = (lax.axis_size(axis), array.shape[dim])
        up = [(i, (i + 1) % size) for i in range(size)]
        last = lax.slice_in_dim(array, length - width, length, axis=dim)
        leading = lax.slice_in_dim(array, 0, width, axis=dim)
        edges[dim] = (
            lax.ppermute(last, axis, up),
            lax.ppermute(leading, axis, [(b, a) for a, b in up]),
        )
    done = []
    for _, dim in sides:
        low, high = edges[dim]
        around = [(width, width) if d in done else (0, 0) for d in range(array.ndim)]
        array = jnp.concatenate([jnp.pad(low, around), array, jnp.pad(high, around)], axis=dim)
        done.append(dim)
    return array


def side_by_side(arrays, axis, dim, along):
    widths = [math.prod(a.shape[along:]) for a in arrays]
    both = jnp.concatenate(
        [a.reshape(*a.shape[:along], w) for a, w in zip(arrays, widths)], axis=along
    )
    filled = lax.all_gather(both, axis, axis=dim, tiled=True)
    pieces = jnp.split(filled, [sum(widths[:k]) for k in range(1, len(widths))], axis=along)
    return tuple(
        (b.reshape(*filled.shape[:along], *a.shape[along:]) for a, b in zip(arrays, pieces))
    )


def toeplitz(rows):
    count = rows.shape[-1]
    lagged = jnp.arange(count)[:, None] - jnp.arange(count)[None, :]
    picked = jnp.take(rows, jnp.clip(lagged, 0, count - 1), axis=-1)
    return jnp.where(lagged >= 0, picked, jnp.zeros_like(picked))


def per_device(
    fields,
    inv_jacobian,
    diff_matrix,
    face_interp,
    lift_matrix,
    flux_couple,
    neighbours,
    send_index,
    bound_coef,
    current_coef,
    time_interp,
    current_history,
    group_weight,
    projection,
    kernels,
    pair_dest,
    pair_count,
):
    elements = fields.shape[2]
    listed = send_index.shape[1]
    directions = projection.shape[1]
    packed = jnp.take(fields, send_index.reshape(-1), axis=2)
    extended = padded_2(packed.astype(jnp.bfloat16), ((("patch", "level"), 2),), listed).astype(
        packed.dtype
    )
    own = jnp.einsum("fqn,cne->fcqe", face_interp, fields, precision=HIGH)
    newest = jnp.einsum("c,cqe->eq", current_coef, own[5, :, :, :BE], precision=HIGH)
    newest = newest.reshape(1, -1).astype(jnp.bfloat16)
    currents = jnp.concatenate([current_history[1:], newest], axis=0)
    grads = jnp.einsum("rmn,cne->rcme", diff_matrix, fields, precision=HIGH) * inv_jacobian
    electric = jnp.stack(
        [grads[1, 5] - grads[2, 4], grads[2, 3] - grads[0, 5], grads[0, 4] - grads[1, 3]]
    )
    magnetic = -jnp.stack(
        [grads[1, 2] - grads[2, 1], grads[2, 0] - grads[0, 2], grads[0, 1] - grads[1, 0]]
    )
    volume = jnp.concatenate([electric, magnetic], axis=0)
    owner = lax.axis_index("patch") * lax.axis_size("level") + lax.axis_index("level")
    shard_currents, shard_weights, shard_projection = side_by_side(
        (currents[None], group_weight[None], projection[None]), ("patch", "level"), 0, 1
    )
    row = lax.dynamic_index_in_dim(shard_weights, owner, 1, keepdims=False)
    weighted = (shard_currents.astype(jnp.float32) * row.astype(jnp.float32)[:, None, :]).astype(
        jnp.bfloat16
    )
    rays = jnp.einsum("ntb,nbk->tk", weighted, shard_projection, preferred_element_type=jnp.float32)
    rays = rays.astype(jnp.bfloat16)
    patches = lax.axis_size("patch")
    pairs = pair_dest.shape[2]
    live = jnp.arange(pairs) < pair_count[0, 0]
    slots = (pair_dest[0, 0][None, :] == jnp.arange(patches)[:, None]) & live[None, :]
    table = jnp.dot(
        slots.astype(jnp.float32), kernels[0, 0].astype(jnp.float32), precision=HIGH
    ).astype(jnp.bfloat16)
    blocks = jnp.einsum("dts,sk->dtk", toeplitz(table), rays, preferred_element_type=jnp.float32)
    received = lax.all_to_all(blocks, "patch", split_axis=0, concat_axis=0, tiled=True)
    incoming = jnp.sum(received, axis=0)
    incoming = incoming.astype(jnp.bfloat16)
    image = jnp.einsum(
        "ntk,bk->ntb",
        lax.all_gather(incoming[None], ("patch", "level"), axis=0, tiled=True),
        projection,
        preferred_element_type=jnp.float32,
    )
    boundary_field = jnp.einsum(
        "ntb,nb->tb", image, group_weight.astype(jnp.float32), precision=HIGH
    )
    boundary_field = boundary_field * (1.0 / jnp.sqrt(jnp.float32(directions)))
    ghosts = jnp.concatenate([extended[:, :, :listed], extended[:, :, 3 * listed :]], axis=2)
    pool = jnp.concatenate([fields, ghosts], axis=2)
    opposite = face_interp[jnp.array([1, 0, 3, 2, 5, 4])]
    across = pool[:, :, neighbours]
    neighbour = jnp.einsum("fqn,cnfe->fcqe", opposite, across, precision=HIGH)
    interp = jnp.dot(time_interp, boundary_field, precision=HIGH).reshape(BE, NFP)
    exterior = bound_coef[:, None, None] * interp.T[None]
    padded = jnp.pad(exterior, ((0, 0), (0, 0), (0, elements - BE)))
    isbound = (jnp.arange(6)[:, None, None, None] == 5) & (
        jnp.arange(elements)[None, None, None, :] < BE
    )
    neighbour = jnp.where(isbound, padded[None], neighbour)
    flux = jnp.einsum("fcd,fdqe->fcqe", flux_couple, neighbour - own, precision=HIGH)
    surface = jnp.einsum("fnq,fcqe->cne", lift_matrix, flux, precision=HIGH)
    return (volume + surface, boundary_field)


def solution(mesh):
    placed = (
        P(None, None, ("patch", "level")),
        P(("patch", "level")),
        P(),
        P(),
        P(),
        P(),
        P(None, ("patch", "level")),
        P(None, ("patch", "level")),
        P(),
        P(),
        P(),
        P(None, ("patch", "level")),
        P(None, ("patch", "level")),
        P(("patch", "level"), None),
        P("level", "patch", None, None),
        P("level", "patch", None),
        P("level", "patch"),
    )
    return jax.shard_map(
        per_device,
        mesh=mesh,
        in_specs=placed,
        out_specs=(P(None, None, ("patch", "level")), P(None, ("patch", "level"))),
        check_vma=False,
    )
```

profile of v0, /device:TPU:1, one launch (start us, length us, event | category | flops | bytes accessed | tf_op | source)
XLA Modules:
  0.0 635.7 jit_solution(1498488128393288354)
XLA Ops:
  7.2 1.6 convolution_bitcast_fusion.1
  10.5 1.1 copy.98
  12.5 1.1 maximum_bitcast_fusion
  15.4 12.1 %gather_fusion = bf16[4096,32]{1,0:T(8,128)(2,1)S(1)} fusion(bf16[32,64]{0,1:T(8,128)(2,1)S(1)} %copy.59, s32[4096]{0:T(1024)S(1)} %broadcast_clamp_fusion), kind=kCustom, calls=%fused_computation | custom fusion | bytes 540672 | tf_op jit(solution)/shard_map/jit(_take)/gather | solution.py:47
  28.5 247.4 %all-gather.7.cloned.1.call-done = bf16[128,1,90112]{2,1,0:T(2,128)(2,1)} async-done(((bf16[1,1,90112]{2,1,0:T(2,128)(2,1)}), bf16[128,1,90112]{2,1,0:T(2,128)(2,1)}) %all-gather.7.cloned.1.call-update) | async-done | bytes 23068688 | tf_op jit(solution)/shard_map/all_gather | solution.py:37
  275.9 39.5 %copy.117 = bf16[128,1,90112]{2,0,1:T(8,128)(2,1)} copy(bf16[128,1,90112]{2,1,0:T(2,128)(2,1)} %all-gather.7.cloned.1.call-done) | data formatting | bytes 46137344
  315.4 2.5 slice_bitcast_fusion
  317.9 2.0 convert_bitcast_fusion
  319.9 8.0 %split.14 = bf16[128,65536]{1,0:T(8,128)(2,1)S(1)} slice(bf16[128,90112]{1,0:T(8,128)(2,1)} %bitcast.199), slice={[0:128], [24576:90112]} | slice | bytes 33554432 | tf_op jit(solution)/shard_map/split | solution.py:38
  327.9 3.2 copy.100
  331.8 8.8 %copy.101 = bf16[16,8,128,512]{3,2,1,0:T(8,128)(2,1)} copy(bf16[16,8,128,512]{3,1,2,0:T(8,128)(2,1)S(1)} %bitcast.201) | data formatting | bytes 33554432
  340.6 1.0 dynamic-slice_convert_fusion
  342.2 9.7 %fusion.16 = f32[32,64,512]{2,1,0:T(8,128)} fusion(bf16[128,64,128]{2,1,0:T(8,128)(2,1)S(1)} %fusion.2, bf16[128,128,512]{2,1,0:T(8,128)(2,1)} %bitcast.200, bf16[64,64,32]{1,0,2:T(8,128)(2,1)S(1)} %copy.60, pred[64,64]{1,0:T(8,128)(4,1)S(1)} %get-tuple-element.11, pred[64,64]{1,0:T(8,128)(4,1)S(1)} %get-tuple-element.12), kind=kOutput, calls=%fused_computation.25 | convolution fusion | flops 1208254464 | bytes 23339008 | tf_op jit(solution)/shard_map/dts,sk->dtk/dot_general | solution.py:106
  352.0 56.3 %all_to_all.5 = f32[32,64,512]{2,1,0:T(8,128)} all-to-all(f32[32,64,512]{2,1,0:T(8,128)} %fusion.16), channel_id=1, replica_groups=mesh['patch'=32,'level'=4] {'patch'}, dimensions={0} | all-to-all | bytes 8388608 | tf_op jit(solution)/shard_map/all_to_all | solution.py:107
  408.3 3.2 reduce_sum.9
  412.9 4.7 collective-permute-start
  418.3 1.1 fusion.3
  420.8 2.0 collective-permute-done.1
  423.0 5.8 gather_fusion.2
  428.8 183.8 %all-gather.5.cloned.1.call-done = bf16[8192,512]{1,0:T(8,128)(2,1)} async-done(((bf16[64,512]{1,0:T(8,128)(2,1)}), bf16[8192,512]{1,0:T(8,128)(2,1)}) %all-gather.5.cloned.1.call-update) | async-done | bytes 8388624 | tf_op jit(solution)/shard_map/all_gather | solution.py:112
  612.6 5.8 multiply_reduce_fusion
  618.8 7.4 %fusion.10 = f32[6,6,16,256]{3,2,0,1:T(8,128)S(1)} fusion(f32[6,6,16,256]{3,2,0,1:T(8,128)S(1)} %convolution_bitcast_fusion.1, f32[6,64,6,256]{1,0,3,2:T(8,128)} %bitcast.202, f32[6,16,256]{2,1,0:T(8,128)S(1)} %pad.4, pred[6,256]{1,0:T(8,128)(4,1)S(1)} %copy-done.8, f32[6,16,64]{2,1,0:T(8,128)S(1)} %gather_fusion.3), kind=kOutput, calls=%fused_computation.18 | convolution fusion | flops 113541120 | bytes 3663360 | tf_op jit(solution)/shard_map/fqn,cnfe->fcqe/dot_general | solution.py:124
  626.2 1.1 convolution_bitcast_fusion
  627.4 1.5 fusion.13
  (82 shorter events, 9.9 us)
Async XLA Ops:
  7.2 411.1 %copy-start = (f32[3,64,64]{2,1,0:T(8,128)S(1)}, f32[3,64,64]{2,1,0:T(8,128)}, u32[]{:S(2)}) copy-start(f32[3,64,64]{2,1,0:T(8,128)} %param.20) | copy-start | bytes 147460
  7.2 268.7 %all-gather.7.cloned.1.call-start = ((), (), s32[]{:S(2)}) async-start(), calls=%async_computation.2 | async-start | bytes 46497792 | tf_op jit(solution)/shard_map/all_gather | solution.py:37
  13.6 599.0 %all-gather.5.cloned.1.call-start = ((), (), s32[]{:S(2)}) async-start(), calls=%async_computation.1 | async-start | bytes 8454144 | tf_op jit(solution)/shard_map/all_gather | solution.py:112
  408.3 3.3 copy-start.1
  408.3 3.7 copy-start.14
  408.3 9.4 %copy-start.9 = (s32[6,256]{1,0:T(8,128)S(1)}, s32[6,256]{1,0:T(8,128)}, u32[]{:S(2)}) copy-start(s32[6,256]{1,0:T(8,128)} %param.24) | copy-start | bytes 18436
  408.3 10.0 %copy-start.10 = (f32[256]{0:T(256)S(1)}, f32[256]{0:T(256)}, u32[]{:S(2)}) copy-start(f32[256]{0:T(256)} %param.19) | copy-start | bytes 3076
  408.3 11.9 %copy-start.4 = (bf16[128,128]{1,0:T(8,128)(2,1)S(1)}, bf16[128,128]{1,0:T(8,128)(2,1)}, u32[]{:S(2)}) copy-start(bf16[128,128]{1,0:T(8,128)(2,1)} %param.30) | copy-start | bytes 98308
  408.3 11.9 %copy-start.13 = (s32[6]{0:T(128)S(1)}, s32[6]{0:T(128)}, u32[]{:S(2)}) copy-start(s32[6]{0:T(128)} %constant.80) | copy-start | bytes 76
  408.3 11.9 %copy-start.2 = (f32[6,16,64]{2,1,0:T(8,128)S(1)}, f32[6,16,64]{2,1,0:T(8,128)}, u32[]{:S(2)}) copy-start(f32[6,16,64]{2,1,0:T(8,128)} %param.21) | copy-start | bytes 73732
  412.9 7.8 %collective-permute-start = (bf16[6,64,16]{1,0,2:T(8,128)(2,1)S(1)}, bf16[6,64,16]{1,0,2:T(8,128)(2,1)S(1)}, u32[]{:S(2)}, u32[]{:S(2)}) collective-permute-start(bf16[6,64,16]{1,0,2:T(8,128)(2,1)S(1)} %get-tuple-element.9), channel_id=1, source_target_pairs={{0,1},{1,2},{2,3},{3,4},{4,5},{5,6},{6,7},{7,8},{8,9},{9,10},{10,1... | collective-permute-start | bytes 36872 | tf_op jit(solution)/shard_map/ppermute | solution.py:20
  417.7 5.1 collective-permute-start.1
  422.8 189.8 %copy-start.3 = (bf16[128,512]{1,0:T(8,128)(2,1)S(1)}, bf16[128,512]{1,0:T(8,128)(2,1)}, u32[]{:S(2)}) copy-start(bf16[128,512]{1,0:T(8,128)(2,1)} %param.31) | copy-start | bytes 393220
  612.6 5.8 copy-start.11
  612.6 6.1 copy-start.12
  612.6 6.2 copy-start.8
  618.4 7.8 %copy-start.7 = (f32[6,6,6]{2,1,0:T(8,128)S(1)}, f32[6,6,6]{2,1,0:T(8,128)}, u32[]{:S(2)}) copy-start(f32[6,6,6]{2,1,0:T(8,128)} %param.23) | copy-start | bytes 2596
  618.4 9.0 %copy-start.6 = (f32[6,64,16]{1,2,0:T(8,128)S(1)}, f32[6,64,16]{1,2,0:T(8,128)}, u32[]{:S(2)}) copy-start(f32[6,64,16]{1,2,0:T(8,128)} %param.22) | copy-start | bytes 73732
  618.4 10.4 %copy-start.5 = (f32[64,128]{1,0:T(8,128)}, f32[64,128]{1,0:T(8,128)S(1)}, u32[]{:S(2)}) copy-start(f32[64,128]{1,0:T(8,128)S(1)} %multiply_bitcast_fusion) | copy-start | bytes 98308
Sparse Core Ops, SparseCore 0:
  13.7 262.1 all-gather.6
  411.7 200.8 all-gather.4
where the time goes:
time: 636 us
  waiting for transfers between devices  433 us (68%)
  local copies, waits for them, and re-layouts  86.5 us (14%)
  blocking collectives  56.3 us (9%)
  matrix products  29.1 us (5%)
  between operations  15.1 us (2%)
  other arithmetic  10.5 us (2%)
    all_gather x1, waiting for transfers between devices, side_by_side(): filled = lax.all_gather(both, axis, axis=dim, tiled=True)  247 us
    all_gather x1, waiting for transfers between devices, per_device(): lax.all_gather(incoming[None], ('patch', 'level'), axis=0, tiled=True)  184 us
    unnamed x39, local copies, waits for them, and re-layouts  57.1 us
    all_to_all x1, blocking collectives, per_device(): lax.all_to_all(blocks, 'patch', split_axis=0, concat_axis=0, tiled=True)  56.3 us
    gather x2, local copies, waits for them, and re-layouts, toeplitz(): picked = jnp.take(rows, jnp.clip(lagged, 0, count - 1), axis=-1)  13.1 us
  transfers between devices with their start and end apart: 4, of which 3 were waited for; matrix products, arithmetic and copies ran while one was open for 4% of the time, Pallas kernels for 0%

commit v1 on v0

--- a/solution.py
+++ b/solution.py
@@ -109,7 +109,15 @@
     incoming = incoming.astype(jnp.bfloat16)
     image = jnp.einsum(
         "ntk,bk->ntb",
-        lax.all_gather(incoming[None], ("patch", "level"), axis=0, tiled=True),
+        jnp.concatenate(
+            lax.all_to_all(
+                jnp.stack([incoming[None]] * lax.axis_size(("patch", "level"))),
+                ("patch", "level"),
+                0,
+                0,
+            ),
+            axis=0,
+        ),
         projection,
         preferred_element_type=jnp.float32,
     )

time: 636 us -> 556 us (0.87); the launches traced: 636 us -> 548 us
  waiting for transfers between devices: 433 us -> 335 us
  starting transfers between devices: 4.81 us -> 11.2 us
    all_gather x1 -> x0, waiting for transfers between devices: 184 us -> none  [per_device(): lax.all_gather(incoming[None], ('patch', 'level'), axis=0, tiled=True)]
    ppermute x1, waiting for transfers between devices: 0.01 us -> 83.1 us  [padded_2(): lax.ppermute(last, axis, up)]
    all_to_all x0 -> x1, starting transfers between devices: none -> 7.9 us  [per_device(): lax.all_to_all(jnp.stack([incoming[None]] * lax.axis_size(('patch', 'leve...]
where the time goes in v1:
time: 556 us; the launch traced here: 548 us
  waiting for transfers between devices  335 us (60%)
  local copies, waits for them, and re-layouts  90.8 us (16%)
  blocking collectives  56.3 us (10%)
  matrix products  29.1 us (5%)
  between operations  15.1 us (3%)
  starting transfers between devices  11.2 us (2%)
  other arithmetic  9.89 us (2%)
    all_gather x1, waiting for transfers between devices, side_by_side(): filled = lax.all_gather(both, axis, axis=dim, tiled=True)  248 us
    ppermute x1, waiting for transfers between devices, padded_2(): lax.ppermute(last, axis, up)  83.1 us
    unnamed x39, local copies, waits for them, and re-layouts  57.1 us
    all_to_all x1, blocking collectives, per_device(): lax.all_to_all(blocks, 'patch', split_axis=0, concat_axis=0, tiled=True)  56.3 us
    gather x2, local copies, waits for them, and re-layouts, toeplitz(): picked = jnp.take(rows, jnp.clip(lagged, 0, count - 1), axis=-1)  13.1 us
  transfers between devices with their start and end apart: 4, of which 3 were waited for; matrix products, arithmetic and copies ran while one was open for 4% of the time, Pallas kernels for 0%

profile of v1, /device:TPU:1, one launch (start us, length us, event | category | flops | bytes accessed | tf_op | source)
XLA Modules:
  0.0 547.5 jit_solution(15825027402628239116)
XLA Ops:
  7.2 1.6 convolution_bitcast_fusion.1
  10.5 1.1 copy.117
  12.5 1.1 maximum_bitcast_fusion
  15.3 12.1 %gather_fusion = bf16[4096,32]{1,0:T(8,128)(2,1)S(1)} fusion(bf16[32,64]{0,1:T(8,128)(2,1)S(1)} %copy.78, s32[4096]{0:T(1024)S(1)} %broadcast_clamp_fusion), kind=kCustom, calls=%fused_computation | custom fusion | bytes 540672 | tf_op jit(solution)/shard_map/jit(_take)/gather | solution.py:47
  28.4 247.5 %all-gather.3.cloned.1.call-done = bf16[128,1,90112]{2,1,0:T(2,128)(2,1)} async-done(((bf16[1,1,90112]{2,1,0:T(2,128)(2,1)}), bf16[128,1,90112]{2,1,0:T(2,128)(2,1)}) %all-gather.3.cloned.1.call-update) | async-done | bytes 23068688 | tf_op jit(solution)/shard_map/all_gather | solution.py:37
  276.0 39.5 %copy.136 = bf16[128,1,90112]{2,0,1:T(8,128)(2,1)} copy(bf16[128,1,90112]{2,1,0:T(2,128)(2,1)} %all-gather.3.cloned.1.call-done) | data formatting | bytes 46137344
  315.4 2.5 slice_bitcast_fusion
  317.9 2.0 convert_bitcast_fusion
  320.0 8.0 %split.14 = bf16[128,65536]{1,0:T(8,128)(2,1)S(1)} slice(bf16[128,90112]{1,0:T(8,128)(2,1)} %bitcast.202), slice={[0:128], [24576:90112]} | slice | bytes 33554432 | tf_op jit(solution)/shard_map/split | solution.py:38
  327.9 3.2 copy.119
  331.9 8.7 %copy.120 = bf16[16,8,128,512]{3,2,1,0:T(8,128)(2,1)} copy(bf16[16,8,128,512]{3,1,2,0:T(8,128)(2,1)S(1)} %bitcast.204) | data formatting | bytes 33554432
  342.3 9.7 %fusion.20 = f32[32,64,512]{2,1,0:T(8,128)} fusion(bf16[128,64,128]{2,1,0:T(8,128)(2,1)S(1)} %fusion.4, bf16[128,128,512]{2,1,0:T(8,128)(2,1)} %bitcast.203, bf16[64,64,32]{1,0,2:T(8,128)(2,1)S(1)} %copy.79, pred[64,64]{1,0:T(8,128)(4,1)S(1)} %get-tuple-element.11, pred[64,64]{1,0:T(8,128)(4,1)S(1)} %get-tuple-element.12), kind=kOutput, calls=%fused_computation.27 | convolution fusion | flops 1208254464 | bytes 23339008 | tf_op jit(solution)/shard_map/dts,sk->dtk/dot_general | solution.py:106
  352.0 56.3 %all_to_all.10 = f32[32,64,512]{2,1,0:T(8,128)} all-to-all(f32[32,64,512]{2,1,0:T(8,128)} %fusion.20), channel_id=1, replica_groups=mesh['patch'=32,'level'=4] {'patch'}, dimensions={0} | all-to-all | bytes 8388608 | tf_op jit(solution)/shard_map/all_to_all | solution.py:107
  408.3 2.6 reduce_sum.9
  410.9 4.3 stack.5
  415.2 7.9 %all-to-all-start.1 = ((bf16[128,1,64,512]{3,2,1,0:T(8,128)(2,1)}), bf16[128,1,64,512]{3,2,1,0:T(8,128)(2,1)}, u32[]{:S(2)}, u32[]{:S(2)}) async-start(bf16[128,1,64,512]{3,2,1,0:T(8,128)(2,1)} %stack.5), calls=%async_computation.1 | async-start | bytes 16777216 | tf_op jit(solution)/shard_map/all_to_all | solution.py:113
  424.5 3.2 collective-permute-start
  430.8 83.1 %collective-permute-done = bf16[6,64,16]{1,0,2:T(8,128)(2,1)S(1)} collective-permute-done((bf16[6,64,16]{1,0,2:T(8,128)(2,1)S(1)}, bf16[6,64,16]{1,0,2:T(8,128)(2,1)S(1)}, u32[]{:S(2)}, u32[]{:S(2)}) %collective-permute-start) | collective-permute-done | bytes 12320 | tf_op jit(solution)/shard_map/ppermute | solution.py:20
  513.9 4.5 collective-permute-done.1
  518.6 5.8 %gather_fusion.2 = f32[1536,6,64]{2,1,0:T(8,128)} fusion(f32[6,64,288]{1,0,2:T(8,128)S(1)} %pad_maximum_fusion, s32[2048]{0:T(1024)} %pad_clamp_fusion), kind=kCustom, calls=%fused_computation.2 | custom fusion | bytes 4724736 | tf_op jit(solution)/shard_map/gather | solution.py:131
  524.5 5.8 %multiply_reduce_fusion = f32[128,64]{0,1:T(8,128)S(1)} fusion(bf16[128,1,64,512]{3,2,1,0:T(8,128)(2,1)} %all-to-all-done.1, f32[128,128]{0,1:T(8,128)S(1)} %bitcast_convert_fusion, bf16[128,512]{1,0:T(8,128)(2,1)S(1)} %copy-done.3), kind=kOutput, calls=%fused_computation.12 | convolution fusion | flops 1075830784 | bytes 8617984 | tf_op jit(solution)/shard_map/ntk,bk->ntb/dot_general | solution.py:110
  530.7 7.4 %fusion.14 = f32[6,6,16,256]{3,2,0,1:T(8,128)S(1)} fusion(f32[6,6,16,256]{3,2,0,1:T(8,128)S(1)} %convolution_bitcast_fusion.1, f32[6,64,6,256]{1,0,3,2:T(8,128)} %bitcast.205, f32[6,16,256]{2,1,0:T(8,128)S(1)} %pad.4, pred[6,256]{1,0:T(8,128)(4,1)S(1)} %copy-done.8, f32[6,16,64]{2,1,0:T(8,128)S(1)} %gather_fusion.3), kind=kOutput, calls=%fused_computation.20 | convolution fusion | flops 113541120 | bytes 3663360 | tf_op jit(solution)/shard_map/fqn,cnfe->fcqe/dot_general | solution.py:132
  538.1 1.1 convolution_bitcast_fusion
  539.2 1.5 fusion.17
  (82 shorter events, 11.9 us)
Async XLA Ops:
  7.2 421.2 %copy-start = (f32[3,64,64]{2,1,0:T(8,128)S(1)}, f32[3,64,64]{2,1,0:T(8,128)}, u32[]{:S(2)}) copy-start(f32[3,64,64]{2,1,0:T(8,128)} %param.20) | copy-start | bytes 147460
  7.2 268.8 %all-gather.3.cloned.1.call-start = ((), (), s32[]{:S(2)}) async-start(), calls=%async_computation.2 | async-start | bytes 46497792 | tf_op jit(solution)/shard_map/all_gather | solution.py:37
  415.1 7.9 %copy-start.1 = (f32[6,64,256]{2,1,0:T(8,128)S(1)}, f32[6,64,256]{2,1,0:T(8,128)}, u32[]{:S(2)}) copy-start(f32[6,64,256]{2,1,0:T(8,128)} %param.18) | copy-start | bytes 1179652
  415.1 8.4 %copy-start.14 = (s32[2,16]{1,0:T(2,128)S(1)}, s32[2,16]{1,0:T(2,128)}, u32[]{:S(2)}) copy-start(s32[2,16]{1,0:T(2,128)} %param.25) | copy-start | bytes 388
  415.1 12.5 %copy-start.9 = (s32[6,256]{1,0:T(8,128)S(1)}, s32[6,256]{1,0:T(8,128)}, u32[]{:S(2)}) copy-start(s32[6,256]{1,0:T(8,128)} %param.24) | copy-start | bytes 18436
  415.1 13.2 %copy-start.10 = (f32[256]{0:T(256)S(1)}, f32[256]{0:T(256)}, u32[]{:S(2)}) copy-start(f32[256]{0:T(256)} %param.19) | copy-start | bytes 3076
  415.2 109.3 %all-to-all-start.1 = ((bf16[128,1,64,512]{3,2,1,0:T(8,128)(2,1)}), bf16[128,1,64,512]{3,2,1,0:T(8,128)(2,1)}, u32[]{:S(2)}, u32[]{:S(2)}) async-start(bf16[128,1,64,512]{3,2,1,0:T(8,128)(2,1)} %stack.5), calls=%async_computation.1 | async-start | bytes 16777216 | tf_op jit(solution)/shard_map/all_to_all | solution.py:113
  423.1 7.1 %copy-start.4 = (bf16[128,128]{1,0:T(8,128)(2,1)S(1)}, bf16[128,128]{1,0:T(8,128)(2,1)}, u32[]{:S(2)}) copy-start(bf16[128,128]{1,0:T(8,128)(2,1)} %param.30) | copy-start | bytes 98308
  423.1 7.1 %copy-start.13 = (s32[6]{0:T(128)S(1)}, s32[6]{0:T(128)}, u32[]{:S(2)}) copy-start(s32[6]{0:T(128)} %constant.80) | copy-start | bytes 76
  423.1 7.1 %copy-start.2 = (f32[6,16,64]{2,1,0:T(8,128)S(1)}, f32[6,16,64]{2,1,0:T(8,128)}, u32[]{:S(2)}) copy-start(f32[6,16,64]{2,1,0:T(8,128)} %param.21) | copy-start | bytes 73732
  424.5 89.4 %collective-permute-start = (bf16[6,64,16]{1,0,2:T(8,128)(2,1)S(1)}, bf16[6,64,16]{1,0,2:T(8,128)(2,1)S(1)}, u32[]{:S(2)}, u32[]{:S(2)}) collective-permute-start(bf16[6,64,16]{1,0,2:T(8,128)(2,1)S(1)} %get-tuple-element.9), channel_id=1, source_target_pairs={{0,1},{1,2},{2,3},{3,4},{4,5},{5,6},{6,7},{7,8},{8,9},{9,10},{10,1... | collective-permute-start | bytes 36872 | tf_op jit(solution)/shard_map/ppermute | solution.py:20
  427.7 90.8 %collective-permute-start.1 = (bf16[6,64,16]{1,0,2:T(8,128)(2,1)S(1)}, bf16[6,64,16]{1,0,2:T(8,128)(2,1)S(1)}, u32[]{:S(2)}, u32[]{:S(2)}) collective-permute-start(bf16[6,64,16]{1,0,2:T(8,128)(2,1)S(1)} %get-tuple-element.10), channel_id=1, source_target_pairs={{1,0},{2,1},{3,2},{4,3},{5,4},{6,5},{7,6},{8,7},{9,8},{10,9},{11,1... | collective-permute-start | bytes 36872 | tf_op jit(solution)/shard_map/ppermute | solution.py:21
  518.4 6.0 %copy-start.3 = (bf16[128,512]{1,0:T(8,128)(2,1)S(1)}, bf16[128,512]{1,0:T(8,128)(2,1)}, u32[]{:S(2)}) copy-start(bf16[128,512]{1,0:T(8,128)(2,1)} %param.31) | copy-start | bytes 393220
  524.4 5.8 %copy-start.11 = (f32[64]{0:T(128)S(1)}, f32[64]{0:T(128)}, u32[]{:S(2)}) copy-start(f32[64]{0:T(128)} %param.28) | copy-start | bytes 772
  524.5 6.1 %copy-start.12 = (f32[6]{0:T(128)S(1)}, f32[6]{0:T(128)}, u32[]{:S(2)}) copy-start(f32[6]{0:T(128)} %param.26) | copy-start | bytes 76
  524.5 6.2 %copy-start.8 = (pred[6,256]{1,0:T(8,128)(4,1)S(1)}, pred[6,256]{1,0:T(8,128)(4,1)}, u32[]{:S(2)}) copy-start(pred[6,256]{1,0:T(8,128)(4,1)} %broadcast_and_fusion) | copy-start | bytes 4612
  530.2 7.8 %copy-start.7 = (f32[6,6,6]{2,1,0:T(8,128)S(1)}, f32[6,6,6]{2,1,0:T(8,128)}, u32[]{:S(2)}) copy-start(f32[6,6,6]{2,1,0:T(8,128)} %param.23) | copy-start | bytes 2596
  530.2 9.0 %copy-start.6 = (f32[6,64,16]{1,2,0:T(8,128)S(1)}, f32[6,64,16]{1,2,0:T(8,128)}, u32[]{:S(2)}) copy-start(f32[6,64,16]{1,2,0:T(8,128)} %param.22) | copy-start | bytes 73732
  530.3 10.4 %copy-start.5 = (f32[64,128]{1,0:T(8,128)}, f32[64,128]{1,0:T(8,128)S(1)}, u32[]{:S(2)}) copy-start(f32[64,128]{1,0:T(8,128)S(1)} %multiply_bitcast_fusion) | copy-start | bytes 98308
Sparse Core Ops, SparseCore 0:
  13.7 262.1 all-gather.2
